TPU v7x, 512 devices: a whole 4x4x16 slice. The times are simulated.
512 devices in a mesh: gx: 64 (over z, x), gy: 8 (over y, core).
Axes of the slice: x: 4, y: 4, z: 16, core: 2. Of those that a mesh axis runs over, the one named last changes fastest.
Arguments:
- velocity: float32 [3, 512, 384, 256], P(None, 'gx', 'gy'), may hold values from -6 to 6
- pressure: float32 [512, 384, 256], P('gx', 'gy'), may hold values from -6 to 6
- viscosity: float32 [512, 384, 256], P('gx', 'gy'), may hold values from 0.12 to 0.6
- wind_profile: float32 [256], replicated, may hold values from 0.5 to 1.5
- panel_area: float32 [16384], P('gy'), may hold values from 0.5 to 2
- slot_cell: int32 [8, 4096], P('gy', 'gx'), may hold values from 0 to 98303
- slot_panel: int32 [8, 4096], P('gy'), may hold values from -1 to 2047, as said below
- panel_shapes: bfloat16 [16384, 2048], P('gy', 'gx'), may hold values from -0.046875 to 0.046875
- node_shapes: bfloat16 [1024, 2048], P(None, 'gx'), may hold values from -0.125 to 0.125
- damper_node: int32 [512], P('gy'), may hold values from 0 to 1022
- damper_viscous: float32 [512], P('gy'), may hold values from 0.2 to 2
- damper_hysteretic: float32 [512], P('gy'), may hold values from 0.2 to 2
- frequency: float32 [2048], P('gx'), may hold values from 0.2 to 1.8
- damping_ratio: float32 [2048], P('gx'), may hold values from 0.05 to 0.5
- modal_state: float32 [2, 2048], P(None, 'gx'), may hold values from -6 to 6
- damper_state: float32 [512], P('gy'), may hold values from -1 to 1
Outputs:
- velocity_next: float32 [3, 512, 384, 256], P(None, 'gx', 'gy')
- pressure_next: float32 [512, 384, 256], P('gx', 'gy')
- modal_next: float32 [2, 2048], P(None, 'gx')
- damper_next: float32 [512], P('gy')
Inputs may be any that keep to these rules, and one draw needn't show every extreme that they name: `slot_panel`: in every row each panel number 0 to 2047 stands in exactly one slot; every other slot holds -1.
All inputs are finite; a program needn't handle non-finite values.
Results may differ from a plain program's by a relative error of at most 0.0013.
Values may be sent and summed in bfloat16 or wider, within the bound.
A program may use at most 64 MiB of HBM per device.

v0:
```python
import jax
import jax.numpy as jnp
from jax import lax
from jax.sharding import PartitionSpec as P

time_step = 0.1
sound_squared = 1.0
modal_step = 0.5
hysteresis_gain = 1.0
shape_beta = 0.5
shape_gamma = 0.5
spring_rate = 0.5


def padded_2(value, sides, width):
    for axis, dim in sides:
        size, length = (lax.axis_size(axis), value.shape[dim])
        up = [(i, (i + 1) % size) for i in range(size - 1)]
        down = [(j, i) for i, j in up]
        last = lax.slice_in_dim(value, length - width, length, axis=dim)
        first = lax.slice_in_dim(value, 0, width, axis=dim)
        before = lax.ppermute(last, axis, up)
        after = lax.ppermute(first, axis, down)
        value = jnp.concatenate([before, value, after], axis=dim)
    return value


def advance(padded, local_viscosity, wind_profile):
    centre_cells = padded[:, 1:-1, 1:-1, 1:-1]
    ahead_cells = padded[:, 2:, 1:-1, 1:-1]
    behind_cells = padded[:, :-2, 1:-1, 1:-1]
    right_cells = padded[:, 1:-1, 2:, 1:-1]
    left_cells = padded[:, 1:-1, :-2, 1:-1]
    above_cells = padded[:, 1:-1, 1:-1, 2:]
    below_cells = padded[:, 1:-1, 1:-1, :-2]
    slope_stream = 0.5 * (ahead_cells - behind_cells)
    slope_span = 0.5 * (right_cells - left_cells)
    slope_vertical = 0.5 * (above_cells - below_cells)
    laplacian = (
        ahead_cells
        + behind_cells
        + right_cells
        + left_cells
        + above_cells
        + below_cells
        - 6.0 * centre_cells
    )
    pressure_slope = jnp.stack([slope_stream[3], slope_span[3], slope_vertical[3]])
    velocity_new = centre_cells[:3] + time_step * (
        -wind_profile * slope_stream[:3] + local_viscosity * laplacian[:3] - pressure_slope
    )
    pressure_new = centre_cells[3] - time_step * sound_squared * (
        slope_stream[0] + slope_span[1] + slope_vertical[2]
    )
    return jnp.concatenate([velocity_new, pressure_new[None]], axis=0)


def vertical_pad(fields):
    return jnp.pad(fields, ((0, 0), (0, 0), (0, 0), (1, 1)))


def body(
    velocity,
    pressure,
    viscosity,
    wind_profile,
    panel_area,
    slot_cell,
    slot_panel,
    panel_shapes,
    node_shapes,
    damper_node,
    damper_viscous,
    damper_hysteretic,
    frequency,
    damping_ratio,
    modal_state,
    damper_state,
):
    fields = jnp.concatenate([velocity, pressure[None]], axis=0)
    for substep in range(2):
        padded = padded_2(fields, (("gx", 1), ("gy", 2)), 1)
        fields = advance(vertical_pad(padded), viscosity, wind_profile)
    velocity_next = fields[:3]
    pressure_next = fields[3]
    slot_count = slot_cell.shape[1]
    panel_count = panel_area.shape[0]
    flat_pressure = pressure_next.reshape(-1)
    sampled = flat_pressure[slot_cell[0]]
    panel_ids = slot_panel[0]
    own_ids = lax.dynamic_slice_in_dim(panel_ids, lax.axis_index("gx") * slot_count, slot_count)
    safe_ids = jnp.where(own_ids < 0, 0, own_ids)
    own_loads = (panel_area[safe_ids] * sampled).astype(jnp.bfloat16)
    every_load = lax.all_gather(own_loads, "gx", axis=0, tiled=True)
    target = jnp.where(panel_ids < 0, panel_count, panel_ids)
    panel_loads = (
        jnp.zeros((panel_count + 1,), jnp.bfloat16).at[target].set(every_load)[:panel_count]
    )
    panel_part = jnp.dot(panel_loads, panel_shapes, preferred_element_type=jnp.float32)
    node_numbers = jnp.arange(node_shapes.shape[0], dtype=jnp.int32)
    upper_pick = (node_numbers[None, :] == damper_node[:, None] + 1).astype(jnp.float32)
    lower_pick = (node_numbers[None, :] == damper_node[:, None]).astype(jnp.float32)
    selector = (upper_pick - lower_pick).astype(jnp.bfloat16)
    drift_shapes = jnp.dot(selector, node_shapes, preferred_element_type=jnp.float32)
    panel_modal = lax.psum(panel_part, "gy")
    displacement = modal_state[0]
    modal_velocity = modal_state[1]
    hysteresis = damper_state
    for modal_turn in range(2):
        stretch, stretch_rate = lax.psum(
            (
                jnp.dot(drift_shapes, displacement, precision=lax.Precision.HIGHEST),
                jnp.dot(drift_shapes, modal_velocity, precision=lax.Precision.HIGHEST),
            ),
            "gx",
        )
        hysteresis = hysteresis + modal_step * (
            hysteresis_gain * stretch_rate
            - shape_beta * jnp.abs(stretch_rate) * hysteresis
            - shape_gamma * stretch_rate * jnp.abs(hysteresis)
        )
        damper_force = -(
            damper_viscous * stretch_rate + spring_rate * stretch + damper_hysteretic * hysteresis
        )
        generalized = jnp.dot(damper_force, drift_shapes, precision=lax.Precision.HIGHEST)
        modal_load = panel_modal + lax.psum(generalized, "gy")
        acceleration = (
            modal_load
            - 2.0 * damping_ratio * frequency * modal_velocity
            - frequency * frequency * displacement
        )
        modal_velocity = modal_velocity + modal_step * acceleration
        displacement = displacement + modal_step * modal_velocity
    return (velocity_next, pressure_next, jnp.stack([displacement, modal_velocity]), hysteresis)


def solution(mesh):
    placed = (
        P(None, "gx", "gy", None),
        P("gx", "gy", None),
        P("gx", "gy", None),
        P(),
        P("gy"),
        P("gy", "gx"),
        P("gy", None),
        P("gy", "gx"),
        P(None, "gx"),
        P("gy"),
        P("gy"),
        P("gy"),
        P("gx"),
        P("gx"),
        P(None, "gx"),
        P("gy"),
    )
    return jax.shard_map(
        body,
        mesh=mesh,
        in_specs=placed,
        out_specs=(P(None, "gx", "gy", None), P("gx", "gy", None), P(None, "gx"), P("gy")),
        check_vma=False,
    )
```

profile of v0, /device:TPU:387, one launch (start us, length us, event | category | flops | bytes accessed | tf_op | source)
XLA Modules:
  0.0 556.4 jit_solution(17609832479686283415)
XLA Ops:
  0.6 0.0 copy-start
  0.7 1.1 fusion.21
  1.9 0.0 copy-start.20
  1.9 3.1 collective-permute-start.1
  5.0 2.2 collective-permute-start
  7.2 0.2 fusion.23
  7.4 0.0 copy-done.12
  7.5 0.1 convolution_bitcast_fusion.4
  7.6 0.1 convolution_bitcast_fusion.5
  7.8 1.7 collective-permute-done.1
  9.5 2.8 collective-permute-done
  12.3 0.1 pad_maximum_fusion.30
  12.4 5.0 collective-permute-start.3
  17.4 1.9 collective-permute-start.2
  19.3 112.8 %all-reduce.4 = (f32[64]{0:T(128)S(1)}, f32[64]{0:T(128)S(1)}) all-reduce(f32[64]{0:T(128)S(1)} %convolution_bitcast_fusion.4, f32[64]{0:T(128)S(1)} %convolution_bitcast_fusion.5), channel_id=1, replica_groups=mesh['gx'=64,'gy'=8] {'gx'}, use_global_device_ids=true, to_apply=%region_3.4 | all-reduce | flops 128 | bytes 1024 | tf_op jit(solution)/shard_map/psum | solution.py:110
  132.2 0.0 collective-permute-done.3
  132.2 3.5 select_maximum_fusion.5
  135.7 0.7 subtract_multiply_fusion.3
  136.4 1.2 subtract_multiply_fusion.5
  137.6 0.0 copy-start.10
  137.6 0.2 bitcast_subtract_fusion.1
  137.8 0.9 copy-done.8
  138.7 0.5 copy-done.4
  139.3 1.2 fusion.13
  140.5 0.0 copy-start.14
  140.5 0.0 copy-start.15
  140.5 0.0 copy-start.16
  140.6 0.0 copy-start.1
  140.6 3.5 collective-permute-start.5
  144.2 5.2 collective-permute-start.4
  149.4 0.1 fusion.28
  149.5 0.1 convolution_bitcast_fusion.3
  149.6 0.9 collective-permute-done.5
  150.5 1.5 collective-permute-done.4
  152.0 0.1 pad_maximum_fusion.26
  152.1 32.2 %collective-permute-start.7 = (f32[4,10,1,256]{3,2,1,0:T(1,128)S(1)}, f32[4,10,1,256]{3,2,1,0:T(1,128)S(1)}, u32[]{:S(2)}, u32[]{:S(2)}) collective-permute-start(f32[4,10,1,256]{3,2,1,0:T(1,128)S(1)} %get-tuple-element.33), channel_id=1, source_target_pairs={{0,1},{1,2},{2,3},{3,4},{4,5},{5,6},{6,7},{8,9},{9,10},{10,11},{11... | collective-permute-start | bytes 122888 | tf_op jit(solution)/shard_map/ppermute | solution.py:22
  184.2 1.9 collective-permute-start.6
  186.2 1.3 dynamic-slice.1
  188.1 0.8 gather_fusion
  188.9 0.7 collective-permute-done.6
  189.5 3.5 select_maximum_fusion
  193.0 2.3 subtract_multiply_fusion
  195.4 0.8 slice.230
  196.1 3.0 subtract_multiply_fusion.2
  199.2 0.0 copy-start.19
  199.2 2.4 fusion.17
  201.6 0.0 copy-start.11
  201.6 0.7 copy-done.11
  202.3 0.9 copy.20
  203.3 1.8 gather_fusion.1
  205.0 0.2 dynamic-update-slice
  205.3 118.6 %all-reduce.2 = bf16[4096]{0:T(1024)(128)(2,1)S(1)} all-reduce(bf16[4096]{0:T(1024)(128)(2,1)S(1)} %dynamic-update-slice), channel_id=1, replica_groups=mesh['gx'=64,'gy'=8] {'gx'}, use_global_device_ids=true, to_apply=%add.2 | all-reduce | flops 4096 | bytes 16384
  323.9 28.6 %scatter_custom_fusion = bf16[2049]{0:T(1024)(128)(2,1)S(1)} fusion(s32[4096]{0:T(1024)S(1)} %bitcast.100, bf16[4096]{0:T(1024)(128)(2,1)S(1)} %all-reduce.2, bf16[]{:T(256)} %constant.19.clone.1), kind=kCustom, calls=%fused_computation.120 | custom fusion | bytes 4100 | tf_op jit(solution)/shard_map/scatter | solution.py:97
  352.5 0.1 convolution_bitcast_fusion.6
  352.6 39.3 %all-reduce.5 = (f32[32]{0:T(128)S(1)}, f32[32]{0:T(128)S(1)}) all-reduce(f32[32]{0:T(128)S(1)} %convolution_bitcast_fusion.6, f32[32]{0:T(128)S(1)} %convolution_bitcast_fusion.3), channel_id=1, replica_groups=mesh['gx'=64,'gy'=8] {'gy'}, use_global_device_ids=true, to_apply=%region_1.2 | all-reduce | flops 64 | bytes 512 | tf_op jit(solution)/shard_map/psum | solution.py:105
  392.0 0.1 convolution_bitcast_fusion.2
  392.1 0.1 convolution_bitcast_fusion.1
  392.2 1.8 slice.229
  394.0 0.8 slice.228
  394.8 115.8 %all-reduce.3 = (f32[64]{0:T(128)S(1)}, f32[64]{0:T(128)S(1)}) all-reduce(f32[64]{0:T(128)S(1)} %convolution_bitcast_fusion.2, f32[64]{0:T(128)S(1)} %convolution_bitcast_fusion.1), channel_id=1, replica_groups=mesh['gx'=64,'gy'=8] {'gx'}, use_global_device_ids=true, to_apply=%region_5.6 | all-reduce | flops 128 | bytes 1024 | tf_op jit(solution)/shard_map/psum | solution.py:110
  510.6 0.1 convolution_bitcast_fusion
  510.8 39.4 %psum.55 = f32[32]{0:T(128)S(1)} all-reduce(f32[32]{0:T(128)S(1)} %convolution_bitcast_fusion), channel_id=1, replica_groups=mesh['gx'=64,'gy'=8] {'gy'}, use_global_device_ids=true, to_apply=%region_7.8 | all-reduce | flops 32 | bytes 256 | tf_op jit(solution)/shard_map/psum | solution.py:126
  550.2 0.6 pad_maximum_fusion.34
  550.8 5.7 %fusion.6 = f32[3,8,48,256]{3,2,1,0:T(8,128)} fusion(f32[3,8,48,256]{3,2,1,0:T(8,128)S(1)} %fusion.13, f32[4,8,48,256]{3,2,1,0:T(8,128)} %get-tuple-element.26, f32[1,8,48,256]{3,2,1,0:T(8,128)S(1)} %get-tuple-element.42, f32[4,8,48,256]{3,2,1,0:T(8,128)} %get-tuple-element.25, f32[4,8,48,256]{3,2,1,0:T(8,128)} %get-tuple-element.31, ...), kind=kLoop, calls=%fused_computation.60 | loop fusion | flops 4718592 | bytes 12583936 | tf_op jit(solution)/shard_map/add | solution.py:49
  (51 shorter events, 0.2 us)
Async XLA Ops:
  0.6 351.8 %copy-start = (bf16[2048,32]{0,1:T(8,128)(2,1)S(1)}, bf16[2048,32]{0,1:T(8,128)(2,1)}, u32[]{:S(2)}) copy-start(bf16[2048,32]{0,1:T(8,128)(2,1)} %param.23) | copy-start | bytes 393220
  0.6 11.7 %copy-start.2 = (f32[3,8,48,256]{3,2,1,0:T(8,128)S(1)}, f32[3,8,48,256]{3,2,1,0:T(8,128)}, u32[]{:S(2)}) copy-start(f32[3,8,48,256]{3,2,1,0:T(8,128)} %param.16) | copy-start | bytes 3538948
  0.7 11.7 %copy-start.3 = (f32[8,48,256]{2,1,0:T(8,128)S(1)}, f32[8,48,256]{2,1,0:T(8,128)}, u32[]{:S(2)}) copy-start(f32[8,48,256]{2,1,0:T(8,128)} %param.17) | copy-start | bytes 1179652
  0.7 6.5 %copy-start.22 = (s32[64]{0:T(128)S(1)}, s32[64]{0:T(128)}, u32[]{:S(2)}) copy-start(s32[64]{0:T(128)} %param.25) | copy-start | bytes 772
  0.7 6.5 %copy-start.21 = (bf16[1024,32]{0,1:T(8,128)(2,1)S(1)}, bf16[1024,32]{0,1:T(8,128)(2,1)}, u32[]{:S(2)}) copy-start(bf16[1024,32]{0,1:T(8,128)(2,1)} %param.24) | copy-start | bytes 196612
  0.7 6.8 %copy-start.12 = (f32[2,32]{1,0:T(2,128)S(1)}, f32[2,32]{1,0:T(2,128)}, u32[]{:S(2)}) copy-start(f32[2,32]{1,0:T(2,128)} %param.30) | copy-start | bytes 772
  0.7 7.0 %copy-start.13 = (s32[1,4096]{1,0:T(1,128)S(1)}, s32[1,4096]{1,0:T(1,128)}, u32[]{:S(2)}) copy-start(s32[1,4096]{1,0:T(1,128)} %param.22) | copy-start | bytes 49156
  0.7 7.1 %copy-start.23 = (s32[1,64]{1,0:T(1,128)S(1)}, s32[1,64]{1,0:T(1,128)}, u32[]{:S(2)}) copy-start(s32[1,64]{1,0:T(1,128)} %param.21) | copy-start | bytes 772
  1.9 17.5 %copy-start.20 = (f32[256]{0:T(256)S(1)}, f32[256]{0:T(256)}, u32[]{:S(2)}) copy-start(f32[256]{0:T(256)} %param.19) | copy-start | bytes 3076
  1.9 7.7 %collective-permute-start.1 = (f32[4,1,48,256]{3,2,1,0:T(8,128)S(1)}, f32[4,1,48,256]{3,2,1,0:T(8,128)S(1)}, u32[]{:S(2)}, u32[]{:S(2)}) collective-permute-start(f32[4,1,48,256]{3,2,1,0:T(8,128)S(1)} %get-tuple-element.46), channel_id=1, source_target_pairs={{0,8},{8,16},{16,24},{24,32},{32,40},{40,48},{48,56},{56,64},{64,7... | collective-permute-start | bytes 589832 | tf_op jit(solution)/shard_map/ppermute | solution.py:22
  5.0 7.3 %collective-permute-start = (f32[4,1,48,256]{3,2,1,0:T(8,128)S(1)}, f32[4,1,48,256]{3,2,1,0:T(8,128)S(1)}, u32[]{:S(2)}, u32[]{:S(2)}) collective-permute-start(f32[4,1,48,256]{3,2,1,0:T(8,128)S(1)} %get-tuple-element.47), channel_id=1, source_target_pairs={{8,0},{16,8},{24,16},{32,24},{40,32},{48,40},{56,48},{64,56},{72,6... | collective-permute-start | bytes 589832 | tf_op jit(solution)/shard_map/ppermute | solution.py:23
  12.4 119.7 %collective-permute-start.3 = (f32[4,10,1,256]{3,2,1,0:T(1,128)S(1)}, f32[4,10,1,256]{3,2,1,0:T(1,128)S(1)}, u32[]{:S(2)}, u32[]{:S(2)}) collective-permute-start(f32[4,10,1,256]{3,2,1,0:T(1,128)S(1)} %get-tuple-element.38), channel_id=1, source_target_pairs={{0,1},{1,2},{2,3},{3,4},{4,5},{5,6},{6,7},{8,9},{9,10},{10,11},{11... | collective-permute-start | bytes 122888 | tf_op jit(solution)/shard_map/ppermute | solution.py:22
  17.4 114.8 %collective-permute-start.2 = (f32[4,10,1,256]{3,2,1,0:T(1,128)S(1)}, f32[4,10,1,256]{3,2,1,0:T(1,128)S(1)}, u32[]{:S(2)}, u32[]{:S(2)}) collective-permute-start(f32[4,10,1,256]{3,2,1,0:T(1,128)S(1)} %get-tuple-element.39), channel_id=1, source_target_pairs={{1,0},{2,1},{3,2},{4,3},{5,4},{6,5},{7,6},{9,8},{10,9},{11,10},{12... | collective-permute-start | bytes 122888 | tf_op jit(solution)/shard_map/ppermute | solution.py:23
  136.4 1.2 copy-start.7
  137.5 1.2 copy-start.8
  137.6 1.7 copy-start.4
  137.6 1.7 copy-start.10
  140.5 9.0 %copy-start.14 = (f32[64]{0:T(128)S(1)}, f32[64]{0:T(128)}, u32[]{:S(2)}) copy-start(f32[64]{0:T(128)} %param.27) | copy-start | bytes 772
  140.5 9.0 %copy-start.15 = (f32[64]{0:T(128)S(1)}, f32[64]{0:T(128)}, u32[]{:S(2)}) copy-start(f32[64]{0:T(128)} %param.26) | copy-start | bytes 772
  140.5 8.9 %copy-start.16 = (f32[64]{0:T(128)S(1)}, f32[64]{0:T(128)}, u32[]{:S(2)}) copy-start(f32[64]{0:T(128)} %param.31) | copy-start | bytes 772
  140.6 47.5 %copy-start.1 = (f32[2048]{0:T(1024)S(1)}, f32[2048]{0:T(1024)}, u32[]{:S(2)}) copy-start(f32[2048]{0:T(1024)} %param.20) | copy-start | bytes 24580
  140.6 9.9 %collective-permute-start.5 = (f32[4,1,48,256]{3,2,1,0:T(8,128)S(1)}, f32[4,1,48,256]{3,2,1,0:T(8,128)S(1)}, u32[]{:S(2)}, u32[]{:S(2)}) collective-permute-start(f32[4,1,48,256]{3,2,1,0:T(8,128)S(1)} %get-tuple-element.40), channel_id=1, source_target_pairs={{0,8},{8,16},{16,24},{24,32},{32,40},{40,48},{48,56},{56,64},{64,7... | collective-permute-start | bytes 589832 | tf_op jit(solution)/shard_map/ppermute | solution.py:22
  144.2 7.8 %collective-permute-start.4 = (f32[4,1,48,256]{3,2,1,0:T(8,128)S(1)}, f32[4,1,48,256]{3,2,1,0:T(8,128)S(1)}, u32[]{:S(2)}, u32[]{:S(2)}) collective-permute-start(f32[4,1,48,256]{3,2,1,0:T(8,128)S(1)} %get-tuple-element.41), channel_id=1, source_target_pairs={{8,0},{16,8},{24,16},{32,24},{40,32},{48,40},{56,48},{64,56},{72,6... | collective-permute-start | bytes 589832 | tf_op jit(solution)/shard_map/ppermute | solution.py:23
  152.1 36.8 %collective-permute-start.7 = (f32[4,10,1,256]{3,2,1,0:T(1,128)S(1)}, f32[4,10,1,256]{3,2,1,0:T(1,128)S(1)}, u32[]{:S(2)}, u32[]{:S(2)}) collective-permute-start(f32[4,10,1,256]{3,2,1,0:T(1,128)S(1)} %get-tuple-element.33), channel_id=1, source_target_pairs={{0,1},{1,2},{2,3},{3,4},{4,5},{5,6},{6,7},{8,9},{9,10},{10,11},{11... | collective-permute-start | bytes 122888 | tf_op jit(solution)/shard_map/ppermute | solution.py:22
  184.2 5.3 collective-permute-start.6
  199.2 2.4 copy-start.5
  199.2 2.4 copy-start.9
  199.2 192.8 %copy-start.18 = (f32[32]{0:T(128)S(1)}, f32[32]{0:T(128)}, u32[]{:S(2)}) copy-start(f32[32]{0:T(128)} %param.28) | copy-start | bytes 388
  199.2 192.8 %copy-start.19 = (f32[32]{0:T(128)S(1)}, f32[32]{0:T(128)}, u32[]{:S(2)}) copy-start(f32[32]{0:T(128)} %param.29) | copy-start | bytes 388
  201.6 0.7 copy-start.11
  202.3 191.7 %copy-start.6 = (f32[4,8,48,256]{3,2,1,0:T(8,128)S(1)}, f32[4,8,48,256]{3,2,1,0:T(8,128)}, u32[]{:S(2)}) copy-start(f32[4,8,48,256]{3,2,1,0:T(8,128)} %copy-done.5) | copy-start | bytes 4718596
  510.6 45.8 %copy-start.17 = (f32[64]{0:T(128)}, f32[64]{0:T(128)S(1)}, u32[]{:S(2)}) copy-start(f32[64]{0:T(128)S(1)} %multiply_add_fusion.1) | copy-start | bytes 772
where the time goes:
time: 557 us; the launch traced here: 556 us
  blocking collectives  426 us (76%)
  starting transfers between devices  55 us (10%)
  local copies, waits for them, and re-layouts  39.3 us (7%)
  other arithmetic  25.7 us (5%)
  waiting for transfers between devices  7.58 us (1%)
    psum x2, blocking collectives, body(): lax.psum((jnp.dot(drift_shapes, displacement, precision=lax.Precision.HIG...  229 us
    unnamed x1, blocking collectives  119 us
    ppermute x4, starting transfers between devices, padded_2(): before = lax.ppermute(last, axis, up)  43.8 us
    psum x1, blocking collectives, body(): modal_load = panel_modal + lax.psum(generalized, 'gy')  39.4 us
    psum x1, blocking collectives, body(): panel_modal = lax.psum(panel_part, 'gy')  39.3 us
    scatter x1, local copies, waits for them, and re-layouts, body(): jnp.zeros((panel_count + 1,), jnp.bfloat16).at[target].set(every_load)  28.6 us
    ppermute x4, starting transfers between devices, padded_2(): after = lax.ppermute(first, axis, down)  11.2 us
  transfers between devices with their start and end apart: 8, of which 5 were waited for; matrix products, arithmetic and copies ran while one was open for 1% of the time, Pallas kernels for 0%

commit v1 on v0

--- a/solution.py
+++ b/solution.py
@@ -102,7 +102,7 @@
     lower_pick = (node_numbers[None, :] == damper_node[:, None]).astype(jnp.float32)
     selector = (upper_pick - lower_pick).astype(jnp.bfloat16)
     drift_shapes = jnp.dot(selector, node_shapes, preferred_element_type=jnp.float32)
-    panel_modal = lax.psum(panel_part, "gy")
+    panel_modal = jnp.sum(lax.all_gather(panel_part, "gy"), axis=0)
     displacement = modal_state[0]
     modal_velocity = modal_state[1]
     hysteresis = damper_state

time: 557 us -> 559 us (level)
    unnamed x1 -> x2, blocking collectives: 119 us -> 159 us
    psum x1 -> x0, blocking collectives: 39.3 us -> none  [body(): panel_modal = lax.psum(panel_part, 'gy')]
  transfers between devices with their start and end apart: 8 -> 8, of which waited for: 5 -> 4; matrix products, arithmetic and copies ran while one was open for 1% -> 1% of each run, Pallas kernels for 0% -> 0%
where the time goes in v1:
time: 559 us
  blocking collectives  427 us (76%)
  starting transfers between devices  55 us (10%)
  local copies, waits for them, and re-layouts  40.8 us (7%)
  other arithmetic  25.7 us (5%)
  waiting for transfers between devices  6.93 us (1%)
    psum x2, blocking collectives, body(): lax.psum((jnp.dot(drift_shapes, displacement, precision=lax.Precision.HIG...  229 us
    unnamed x2, blocking collectives  159 us
    ppermute x4, starting transfers between devices, padded_2(): before = lax.ppermute(last, axis, up)  43.8 us
    psum x1, blocking collectives, body(): modal_load = panel_modal + lax.psum(generalized, 'gy')  39.4 us
    scatter x1, local copies, waits for them, and re-layouts, body(): jnp.zeros((panel_count + 1,), jnp.bfloat16).at[target].set(every_load)  28.6 us
    ppermute x4, starting transfers between devices, padded_2(): after = lax.ppermute(first, axis, down)  11.2 us
  transfers between devices with their start and end apart: 8, of which 4 were waited for; matrix products, arithmetic and copies ran while one was open for 1% of the time, Pallas kernels for 0%

profile of v1, /device:TPU:387, one launch (start us, length us, event | category | flops | bytes accessed | tf_op | source)
XLA Modules:
  0.0 558.7 jit_solution(1117556096913941084)
XLA Ops:
  0.6 0.0 copy-start
  0.7 1.1 fusion.21
  1.9 0.0 copy-start.20
  1.9 3.1 collective-permute-start.1
  5.0 2.2 collective-permute-start
  7.2 0.2 fusion.23
  7.4 0.0 copy-done.12
  7.5 0.1 convolution_bitcast_fusion.4
  7.6 0.1 convolution_bitcast_fusion.5
  7.8 1.7 collective-permute-done.1
  9.5 2.8 collective-permute-done
  12.3 0.1 pad_maximum_fusion.30
  12.4 5.0 collective-permute-start.3
  17.4 1.9 collective-permute-start.2
  19.3 112.8 %all-reduce.5 = (f32[64]{0:T(128)S(1)}, f32[64]{0:T(128)S(1)}) all-reduce(f32[64]{0:T(128)S(1)} %convolution_bitcast_fusion.4, f32[64]{0:T(128)S(1)} %convolution_bitcast_fusion.5), channel_id=1, replica_groups=mesh['gx'=64,'gy'=8] {'gx'}, use_global_device_ids=true, to_apply=%region_3.4 | all-reduce | flops 128 | bytes 1024 | tf_op jit(solution)/shard_map/psum | solution.py:110
  132.2 3.5 select_maximum_fusion.5
  135.7 0.7 subtract_multiply_fusion.3
  136.4 1.2 subtract_multiply_fusion.5
  137.6 0.0 copy-start.10
  137.6 0.2 bitcast_subtract_fusion.1
  137.8 0.9 copy-done.8
  138.7 0.5 copy-done.4
  139.3 1.2 fusion.13
  140.5 0.0 copy-start.14
  140.5 0.0 copy-start.15
  140.5 0.0 copy-start.16
  140.6 0.0 copy-start.1
  140.6 3.5 collective-permute-start.5
  144.2 5.2 collective-permute-start.4
  149.4 0.1 fusion.28
  149.5 0.1 convolution_bitcast_fusion.3
  149.6 0.9 collective-permute-done.5
  150.5 1.5 collective-permute-done.4
  152.0 0.1 pad_maximum_fusion.26
  152.1 32.2 %collective-permute-start.7 = (f32[4,10,1,256]{3,2,1,0:T(1,128)S(1)}, f32[4,10,1,256]{3,2,1,0:T(1,128)S(1)}, u32[]{:S(2)}, u32[]{:S(2)}) collective-permute-start(f32[4,10,1,256]{3,2,1,0:T(1,128)S(1)} %get-tuple-element.33), channel_id=1, source_target_pairs={{0,1},{1,2},{2,3},{3,4},{4,5},{5,6},{6,7},{8,9},{9,10},{10,11},{11... | collective-permute-start | bytes 122888 | tf_op jit(solution)/shard_map/ppermute | solution.py:22
  184.2 1.9 collective-permute-start.6
  186.2 1.3 dynamic-slice.2
  187.4 1.3 dynamic-slice.1
  190.0 0.8 gather_fusion
  190.8 3.5 select_maximum_fusion
  194.3 2.3 subtract_multiply_fusion
  196.6 0.8 slice.230
  197.4 3.0 subtract_multiply_fusion.2
  200.5 2.4 fusion.17
  202.9 0.0 copy-start.11
  202.9 0.7 copy-done.11
  203.6 0.9 copy.20
  204.6 1.8 gather_fusion.1
  206.3 0.2 dynamic-update-slice
  206.6 118.3 %all-reduce.2 = bf16[4096]{0:T(1024)(128)(2,1)S(1)} all-reduce(bf16[4096]{0:T(1024)(128)(2,1)S(1)} %dynamic-update-slice), channel_id=1, replica_groups=mesh['gx'=64,'gy'=8] {'gx'}, use_global_device_ids=true, to_apply=%add.2 | all-reduce | flops 4096 | bytes 16384
  324.8 28.6 %scatter_custom_fusion = bf16[2049]{0:T(1024)(128)(2,1)S(1)} fusion(s32[4096]{0:T(1024)S(1)} %bitcast.101, bf16[4096]{0:T(1024)(128)(2,1)S(1)} %all-reduce.2, bf16[]{:T(256)} %constant.19.clone.1), kind=kCustom, calls=%fused_computation.120 | custom fusion | bytes 4100 | tf_op jit(solution)/shard_map/scatter | solution.py:97
  353.4 0.1 convolution_bitcast_fusion.6
  353.6 0.2 dynamic-update-slice.1
  353.8 40.3 %all-reduce.6 = (f32[256]{0:T(256)S(1)}, f32[32]{0:T(128)S(1)}) all-reduce(f32[256]{0:T(256)S(1)} %dynamic-update-slice.1, f32[32]{0:T(128)S(1)} %convolution_bitcast_fusion.3), channel_id=2, replica_groups=mesh['gx'=64,'gy'=8] {'gy'}, use_global_device_ids=true, to_apply=%add.3 | all-reduce | flops 288 | bytes 2304
  394.1 0.1 reshape.136
  394.2 0.1 convolution_bitcast_fusion.2
  394.3 0.1 convolution_bitcast_fusion.1
  394.5 1.8 slice.229
  396.3 0.8 slice.228
  397.0 115.8 %all-reduce.4 = (f32[64]{0:T(128)S(1)}, f32[64]{0:T(128)S(1)}) all-reduce(f32[64]{0:T(128)S(1)} %convolution_bitcast_fusion.2, f32[64]{0:T(128)S(1)} %convolution_bitcast_fusion.1), channel_id=1, replica_groups=mesh['gx'=64,'gy'=8] {'gx'}, use_global_device_ids=true, to_apply=%region_5.6 | all-reduce | flops 128 | bytes 1024 | tf_op jit(solution)/shard_map/psum | solution.py:110
  512.8 0.1 convolution_bitcast_fusion
  513.0 39.4 %psum.47 = f32[32]{0:T(128)S(1)} all-reduce(f32[32]{0:T(128)S(1)} %convolution_bitcast_fusion), channel_id=1, replica_groups=mesh['gx'=64,'gy'=8] {'gy'}, use_global_device_ids=true, to_apply=%region_7.8 | all-reduce | flops 32 | bytes 256 | tf_op jit(solution)/shard_map/psum | solution.py:126
  552.4 0.6 pad_maximum_fusion.34
  553.0 5.7 %fusion.6 = f32[3,8,48,256]{3,2,1,0:T(8,128)} fusion(f32[3,8,48,256]{3,2,1,0:T(8,128)S(1)} %fusion.13, f32[4,8,48,256]{3,2,1,0:T(8,128)} %get-tuple-element.26, f32[1,8,48,256]{3,2,1,0:T(8,128)S(1)} %get-tuple-element.42, f32[4,8,48,256]{3,2,1,0:T(8,128)} %get-tuple-element.25, f32[4,8,48,256]{3,2,1,0:T(8,128)} %get-tuple-element.31, ...), kind=kLoop, calls=%fused_computation.60 | loop fusion | flops 4718592 | bytes 12583936 | tf_op jit(solution)/shard_map/add | solution.py:49
  (56 shorter events, 0.3 us)
Async XLA Ops:
  0.6 352.8 %copy-start = (bf16[2048,32]{0,1:T(8,128)(2,1)S(1)}, bf16[2048,32]{0,1:T(8,128)(2,1)}, u32[]{:S(2)}) copy-start(bf16[2048,32]{0,1:T(8,128)(2,1)} %param.23) | copy-start | bytes 393220
  0.6 11.7 %copy-start.2 = (f32[3,8,48,256]{3,2,1,0:T(8,128)S(1)}, f32[3,8,48,256]{3,2,1,0:T(8,128)}, u32[]{:S(2)}) copy-start(f32[3,8,48,256]{3,2,1,0:T(8,128)} %param.16) | copy-start | bytes 3538948
  0.7 11.7 %copy-start.3 = (f32[8,48,256]{2,1,0:T(8,128)S(1)}, f32[8,48,256]{2,1,0:T(8,128)}, u32[]{:S(2)}) copy-start(f32[8,48,256]{2,1,0:T(8,128)} %param.17) | copy-start | bytes 1179652
  0.7 6.5 %copy-start.22 = (s32[64]{0:T(128)S(1)}, s32[64]{0:T(128)}, u32[]{:S(2)}) copy-start(s32[64]{0:T(128)} %param.25) | copy-start | bytes 772
  0.7 6.5 %copy-start.21 = (bf16[1024,32]{0,1:T(8,128)(2,1)S(1)}, bf16[1024,32]{0,1:T(8,128)(2,1)}, u32[]{:S(2)}) copy-start(bf16[1024,32]{0,1:T(8,128)(2,1)} %param.24) | copy-start | bytes 196612
  0.7 6.8 %copy-start.12 = (f32[2,32]{1,0:T(2,128)S(1)}, f32[2,32]{1,0:T(2,128)}, u32[]{:S(2)}) copy-start(f32[2,32]{1,0:T(2,128)} %param.30) | copy-start | bytes 772
  0.7 7.0 %copy-start.13 = (s32[1,4096]{1,0:T(1,128)S(1)}, s32[1,4096]{1,0:T(1,128)}, u32[]{:S(2)}) copy-start(s32[1,4096]{1,0:T(1,128)} %param.22) | copy-start | bytes 49156
  0.7 7.1 %copy-start.23 = (s32[1,64]{1,0:T(1,128)S(1)}, s32[1,64]{1,0:T(1,128)}, u32[]{:S(2)}) copy-start(s32[1,64]{1,0:T(1,128)} %param.21) | copy-start | bytes 772
  1.9 17.5 %copy-start.20 = (f32[256]{0:T(256)S(1)}, f32[256]{0:T(256)}, u32[]{:S(2)}) copy-start(f32[256]{0:T(256)} %param.19) | copy-start | bytes 3076
  1.9 7.7 %collective-permute-start.1 = (f32[4,1,48,256]{3,2,1,0:T(8,128)S(1)}, f32[4,1,48,256]{3,2,1,0:T(8,128)S(1)}, u32[]{:S(2)}, u32[]{:S(2)}) collective-permute-start(f32[4,1,48,256]{3,2,1,0:T(8,128)S(1)} %get-tuple-element.46), channel_id=1, source_target_pairs={{0,8},{8,16},{16,24},{24,32},{32,40},{40,48},{48,56},{56,64},{64,7... | collective-permute-start | bytes 589832 | tf_op jit(solution)/shard_map/ppermute | solution.py:22
  5.0 7.3 %collective-permute-start = (f32[4,1,48,256]{3,2,1,0:T(8,128)S(1)}, f32[4,1,48,256]{3,2,1,0:T(8,128)S(1)}, u32[]{:S(2)}, u32[]{:S(2)}) collective-permute-start(f32[4,1,48,256]{3,2,1,0:T(8,128)S(1)} %get-tuple-element.47), channel_id=1, source_target_pairs={{8,0},{16,8},{24,16},{32,24},{40,32},{48,40},{56,48},{64,56},{72,6... | collective-permute-start | bytes 589832 | tf_op jit(solution)/shard_map/ppermute | solution.py:23
  12.4 119.7 %collective-permute-start.3 = (f32[4,10,1,256]{3,2,1,0:T(1,128)S(1)}, f32[4,10,1,256]{3,2,1,0:T(1,128)S(1)}, u32[]{:S(2)}, u32[]{:S(2)}) collective-permute-start(f32[4,10,1,256]{3,2,1,0:T(1,128)S(1)} %get-tuple-element.38), channel_id=1, source_target_pairs={{0,1},{1,2},{2,3},{3,4},{4,5},{5,6},{6,7},{8,9},{9,10},{10,11},{11... | collective-permute-start | bytes 122888 | tf_op jit(solution)/shard_map/ppermute | solution.py:22
  17.4 114.8 %collective-permute-start.2 = (f32[4,10,1,256]{3,2,1,0:T(1,128)S(1)}, f32[4,10,1,256]{3,2,1,0:T(1,128)S(1)}, u32[]{:S(2)}, u32[]{:S(2)}) collective-permute-start(f32[4,10,1,256]{3,2,1,0:T(1,128)S(1)} %get-tuple-element.39), channel_id=1, source_target_pairs={{1,0},{2,1},{3,2},{4,3},{5,4},{6,5},{7,6},{9,8},{10,9},{11,10},{12... | collective-permute-start | bytes 122888 | tf_op jit(solution)/shard_map/ppermute | solution.py:23
  136.4 1.2 copy-start.7
  137.5 1.2 copy-start.8
  137.6 1.7 copy-start.4
  137.6 1.7 copy-start.10
  140.5 9.0 %copy-start.14 = (f32[64]{0:T(128)S(1)}, f32[64]{0:T(128)}, u32[]{:S(2)}) copy-start(f32[64]{0:T(128)} %param.27) | copy-start | bytes 772
  140.5 9.0 %copy-start.15 = (f32[64]{0:T(128)S(1)}, f32[64]{0:T(128)}, u32[]{:S(2)}) copy-start(f32[64]{0:T(128)} %param.26) | copy-start | bytes 772
  140.5 8.9 %copy-start.16 = (f32[64]{0:T(128)S(1)}, f32[64]{0:T(128)}, u32[]{:S(2)}) copy-start(f32[64]{0:T(128)} %param.31) | copy-start | bytes 772
  140.6 49.4 %copy-start.1 = (f32[2048]{0:T(1024)S(1)}, f32[2048]{0:T(1024)}, u32[]{:S(2)}) copy-start(f32[2048]{0:T(1024)} %param.20) | copy-start | bytes 24580
  140.6 9.9 %collective-permute-start.5 = (f32[4,1,48,256]{3,2,1,0:T(8,128)S(1)}, f32[4,1,48,256]{3,2,1,0:T(8,128)S(1)}, u32[]{:S(2)}, u32[]{:S(2)}) collective-permute-start(f32[4,1,48,256]{3,2,1,0:T(8,128)S(1)} %get-tuple-element.40), channel_id=1, source_target_pairs={{0,8},{8,16},{16,24},{24,32},{32,40},{40,48},{48,56},{56,64},{64,7... | collective-permute-start | bytes 589832 | tf_op jit(solution)/shard_map/ppermute | solution.py:22
  144.2 7.8 %collective-permute-start.4 = (f32[4,1,48,256]{3,2,1,0:T(8,128)S(1)}, f32[4,1,48,256]{3,2,1,0:T(8,128)S(1)}, u32[]{:S(2)}, u32[]{:S(2)}) collective-permute-start(f32[4,1,48,256]{3,2,1,0:T(8,128)S(1)} %get-tuple-element.41), channel_id=1, source_target_pairs={{8,0},{16,8},{24,16},{32,24},{40,32},{48,40},{56,48},{64,56},{72,6... | collective-permute-start | bytes 589832 | tf_op jit(solution)/shard_map/ppermute | solution.py:23
  152.1 38.7 %collective-permute-start.7 = (f32[4,10,1,256]{3,2,1,0:T(1,128)S(1)}, f32[4,10,1,256]{3,2,1,0:T(1,128)S(1)}, u32[]{:S(2)}, u32[]{:S(2)}) collective-permute-start(f32[4,10,1,256]{3,2,1,0:T(1,128)S(1)} %get-tuple-element.33), channel_id=1, source_target_pairs={{0,1},{1,2},{2,3},{3,4},{4,5},{5,6},{6,7},{8,9},{9,10},{10,11},{11... | collective-permute-start | bytes 122888 | tf_op jit(solution)/shard_map/ppermute | solution.py:22
  184.2 6.6 %collective-permute-start.6 = (f32[4,10,1,256]{3,2,1,0:T(1,128)S(1)}, f32[4,10,1,256]{3,2,1,0:T(1,128)S(1)}, u32[]{:S(2)}, u32[]{:S(2)}) collective-permute-start(f32[4,10,1,256]{3,2,1,0:T(1,128)S(1)} %get-tuple-element.34), channel_id=1, source_target_pairs={{1,0},{2,1},{3,2},{4,3},{5,4},{6,5},{7,6},{9,8},{10,9},{11,10},{12... | collective-permute-start | bytes 122888 | tf_op jit(solution)/shard_map/ppermute | solution.py:23
  200.5 2.4 copy-start.5
  200.5 2.4 copy-start.9
  200.5 193.7 %copy-start.18 = (f32[32]{0:T(128)S(1)}, f32[32]{0:T(128)}, u32[]{:S(2)}) copy-start(f32[32]{0:T(128)} %param.28) | copy-start | bytes 388
  200.5 193.7 %copy-start.19 = (f32[32]{0:T(128)S(1)}, f32[32]{0:T(128)}, u32[]{:S(2)}) copy-start(f32[32]{0:T(128)} %param.29) | copy-start | bytes 388
  202.9 0.7 copy-start.11
  203.6 192.7 %copy-start.6 = (f32[4,8,48,256]{3,2,1,0:T(8,128)S(1)}, f32[4,8,48,256]{3,2,1,0:T(8,128)}, u32[]{:S(2)}) copy-start(f32[4,8,48,256]{3,2,1,0:T(8,128)} %copy-done.5) | copy-start | bytes 4718596
  512.8 45.8 %copy-start.17 = (f32[64]{0:T(128)}, f32[64]{0:T(128)S(1)}, u32[]{:S(2)}) copy-start(f32[64]{0:T(128)S(1)} %multiply_add_fusion.1) | copy-start | bytes 772
